TPU v7x, 1024 devices: a whole 4x8x16 slice. The times are simulated.
1024 devices in a mesh: dp: 64 (over x, y, core), mp: 16 (over z).
Axes of the slice: x: 4, y: 8, z: 16, core: 2. Of those that a mesh axis runs over, the one named last changes fastest.
Arguments:
- patches: bfloat16 [2048, 81920], P('dp', 'mp'), may hold values from -10 to 10
- norm_gain: float32 [1280], replicated, may hold values from 0.1 to 1.9
- qkv_weight: bfloat16 [1280, 3840], P(None, 'mp'), may hold values from -6 to 6
- out_weight: bfloat16 [1280, 1280], P('mp'), may hold values from -0.15625 to 0.15625
- window_plan: int32 [64, 32], replicated, may hold values from -1 to 63, as said below
Outputs:
- attended: bfloat16 [2048, 81920], P('dp', 'mp')
Inputs may be any that keep to these rules, and one draw needn't show every extreme that they name: `window_plan`: each home's live slots come first; over all homes every encoder device is named by exactly 16 slots; one home names one encoder at most 1 times and some home reaches that; the busiest home has all 32 slots live.
All inputs are finite; a program needn't handle non-finite values.
Results may differ from a plain program's by a relative error of at most 0.018.
Values may be sent and summed in bfloat16 or wider, within the bound.
No kernel may reach another device: no remote copies, remote signals or barrier semaphores. Data moves between devices by JAX's collectives and lax.ppermute only.
A program may use at most 128 MiB of HBM per device.

v0:
```python
import jax
import jax.numpy as jnp
from jax import lax
from jax.sharding import PartitionSpec as P

HEAD_DIM = 80
WIN = 64


epsilon = 1e-06


def encode(rows_local, norm_gain, qkv_weight, out_weight):
    full_rows = lax.all_gather(rows_local, "mp", axis=1, tiled=True)
    window_count = full_rows.shape[0]
    full_width = full_rows.shape[1] // WIN
    patch_rows = jnp.transpose(full_rows.reshape(window_count, full_width, WIN), (0, 2, 1))
    patch_rows = patch_rows.reshape(window_count * WIN, full_width)
    as_float = patch_rows.astype(jnp.float32)
    mean_square = jnp.mean(as_float * as_float, axis=-1, keepdims=True)
    normed = (as_float * lax.rsqrt(mean_square + epsilon) * norm_gain).astype(jnp.bfloat16)
    projected = jnp.dot(normed, qkv_weight, preferred_element_type=jnp.float32).astype(jnp.bfloat16)
    heads_here = qkv_weight.shape[1] // (3 * HEAD_DIM)
    projected = projected.reshape(window_count, WIN, heads_here, 3, HEAD_DIM)
    queries = projected[:, :, :, 0, :]
    key_vecs = projected[:, :, :, 1, :]
    value_vecs = projected[:, :, :, 2, :]
    scores = jnp.einsum(
        "wqhd,wkhd->whqk", queries, key_vecs, preferred_element_type=jnp.float32
    ) * HEAD_DIM ** (-0.5)
    attn_weights = jax.nn.softmax(scores, axis=-1).astype(jnp.bfloat16)
    heads_out = jnp.einsum(
        "whqk,wkhd->hdwq", attn_weights, value_vecs, preferred_element_type=jnp.float32
    )
    local_width = heads_here * HEAD_DIM
    heads_out = heads_out.astype(jnp.bfloat16).reshape(local_width, window_count * WIN)
    share_rows = out_weight.shape[1] // lax.axis_size("mp")
    summed = lax.psum_scatter(
        lax.dot_general(
            out_weight, heads_out, (((0,), (0,)), ((), ())), preferred_element_type=jnp.float32
        ).astype(jnp.bfloat16),
        "mp",
        scatter_dimension=0,
        tiled=True,
    ).astype(jnp.float32)
    summed = jnp.transpose(summed.reshape(share_rows, window_count, WIN), (1, 0, 2))
    residual = rows_local.reshape(window_count, share_rows, WIN).astype(jnp.float32)
    block_out = (residual + summed).astype(jnp.bfloat16)
    return block_out.reshape(window_count, share_rows * WIN)


def body(patches, norm_gain, qkv_weight, out_weight, window_plan):
    here_index = lax.axis_index("dp")
    my_plan = lax.dynamic_slice_in_dim(window_plan, here_index, 1, 0)[0]
    is_live = my_plan >= 0
    results = encode(patches, norm_gain, qkv_weight, out_weight)
    results = jnp.where(is_live[:, None], results, jnp.zeros_like(results[:1]))
    return results


def solution(mesh):
    return jax.shard_map(
        body,
        mesh=mesh,
        in_specs=(P("dp", "mp"), P(), P(None, "mp"), P("mp", None), P()),
        out_specs=P("dp", "mp"),
        check_vma=False,
    )
```

profile of v0, /device:TPU:2, one launch (start us, length us, event | category | flops | bytes accessed | tf_op | source)
XLA Modules:
  0.0 309.6 jit_solution(13336624500147170319)
XLA Ops:
  6.5 0.7 all-gather.2.cloned.1.call-update
  7.3 95.0 %all-gather.2.cloned.1.call-done = bf16[32,81920]{1,0:T(8,128)(2,1)} async-done(((bf16[32,5120]{1,0:T(8,128)(2,1)}), bf16[32,81920]{1,0:T(8,128)(2,1)}) %all-gather.2.cloned.1.call-update) | async-done | bytes 5242896 | tf_op jit(solution)/shard_map/all_gather | solution.py:14
  102.3 7.1 %convert_multiply_fusion = f32[32,81920]{1,0:T(8,128)} fusion(bf16[32,81920]{1,0:T(8,128)(2,1)} %all-gather.2.cloned.1.call-done), kind=kLoop, calls=%fused_computation.6 | loop fusion | flops 5242880 | bytes 15728640 | tf_op jit(solution)/shard_map/mul | solution.py:20
  109.4 24.5 %mul.32 = f32[32,1280,64]{2,1,0:T(8,128)} reshape(f32[32,81920]{1,0:T(8,128)} %convert_multiply_fusion) | data formatting | bytes 20971520 | tf_op jit(solution)/shard_map/mul | solution.py:20
  133.9 8.0 %reduce_sum.18 = f32[32,64]{1,0:T(8,128)S(1)} reduce(f32[32,1280,64]{2,1,0:T(8,128)} %mul.32, f32[]{:T(128)} %constant.5.clone.1), dimensions={1}, to_apply=%region_0.0 | reduce | flops 2619392 | bytes 10493956 | tf_op jit(solution)/shard_map/reduce_sum | solution.py:20
  142.1 23.9 %reshape.91 = f32[32,1280,64]{2,1,0:T(8,128)} reshape(bf16[32,81920]{1,0:T(8,128)(2,1)} %all-gather.2.cloned.1.call-done) | data formatting | bytes 15728640 | tf_op jit(solution)/shard_map/convert_element_type | solution.py:19
  166.0 15.7 %copy.30 = f32[32,64,1280]{2,1,0:T(8,128)} copy(f32[32,64,1280]{1,2,0:T(8,128)} %bitcast.43) | data formatting | bytes 20971520 | tf_op jit(solution)/shard_map/convert_element_type | solution.py:19
  181.8 4.9 %fusion.2 = bf16[2048,1280]{1,0:T(8,128)(2,1)S(1)} fusion(f32[32,64,1280]{2,1,0:T(8,128)} %copy.30, f32[1280]{0:T(1024)S(1)} %copy-done.4, f32[2048]{0:T(1024)S(1)} %rsqrt.12), kind=kLoop, calls=%fused_computation.3 | loop fusion | flops 7864320 | bytes 15741952 | tf_op jit(solution)/shard_map/convert_element_type | solution.py:21
  186.7 2.5 convolution_convert_fusion.1
  189.2 3.4 %reshape.81 = bf16[32,64,1,3,80]{1,0,4,3,2:T(8,128)(2,1)S(1)} reshape(bf16[2048,240]{0,1:T(8,128)(2,1)} %convolution_convert_fusion.1) | data formatting | bytes 1966080 | tf_op jit(solution)/shard_map/reshape | solution.py:24
  192.6 1.5 fusion.18
  194.1 1.8 copy.41
  195.9 1.8 copy.42
  197.6 1.4 convolution_multiply_fusion
  199.5 0.7 copy.40
  200.3 2.0 convolution_convert_fusion.2
  202.3 3.9 %fusion.3 = bf16[1280,2048]{0,1:T(8,128)(2,1)} fusion(bf16[80,2048]{0,1:T(8,128)(2,1)S(1)} %bitcast.44, bf16[80,1280]{1,0:T(8,128)(2,1)S(1)} %copy-done.2), kind=kOutput, calls=%fused_computation.5 | convolution fusion | flops 422051840 | bytes 5775360 | tf_op jit(solution)/shard_map/dot_general | solution.py:39
  206.1 7.9 %copy.38 = bf16[1280,2048]{1,0:T(8,128)(2,1)} copy(bf16[1280,2048]{0,1:T(8,128)(2,1)} %fusion.3) | data formatting | bytes 10485760
  214.1 0.9 copy-done.1
  215.6 81.7 %reduce-scatter.4.cloned.1.call-done = bf16[80,2048]{1,0:T(8,128)(2,1)} async-done(((bf16[1280,2048]{1,0:T(8,128)(2,1)}), bf16[80,2048]{1,0:T(8,128)(2,1)}) %reduce-scatter.4.cloned.1.call-update) | async-done | bytes 327696 | tf_op jit(solution)/shard_map/reduce_scatter | solution.py:38
  297.3 1.5 reshape.90
  298.8 1.6 fusion.6
  300.4 1.6 reshape.87
  301.9 0.8 broadcast_select_fusion
  (17 shorter events, 1.2 us)
Async XLA Ops:
  6.5 180.2 %copy-start = (bf16[1280,240]{0,1:T(8,128)(2,1)S(1)}, bf16[1280,240]{0,1:T(8,128)(2,1)}, u32[]{:S(2)}) copy-start(bf16[1280,240]{0,1:T(8,128)(2,1)} %param.7) | copy-start | bytes 1843204
  6.5 95.8 %all-gather.2.cloned.1.call-start = ((), (), s32[]{:S(2)}) async-start(), calls=%async_computation.1 | async-start | bytes 5570560 | tf_op jit(solution)/shard_map/all_gather | solution.py:14
  7.3 290.0 %reduce-scatter.4.cloned.1.call-start = ((), (), s32[]{:S(2)}) async-start(), calls=%async_computation.2 | async-start | bytes 5570560 | tf_op jit(solution)/shard_map/reduce_scatter | solution.py:38
  166.0 15.7 %copy-start.4 = (f32[1280]{0:T(1024)S(1)}, f32[1280]{0:T(1024)}, u32[]{:S(2)}) copy-start(f32[1280]{0:T(1024)} %param.6) | copy-start | bytes 15364
  197.6 4.6 %copy-start.2 = (bf16[80,1280]{1,0:T(8,128)(2,1)S(1)}, bf16[80,1280]{1,0:T(8,128)(2,1)}, u32[]{:S(2)}) copy-start(bf16[80,1280]{1,0:T(8,128)(2,1)} %param.8) | copy-start | bytes 614404
  214.0 1.0 copy-start.1
  214.1 1.3 copy-start.3
Sparse Core Ops, SparseCore 0:
  10.0 92.2 all-gather.1
  214.2 83.0 reduce-scatter.3
where the time goes:
time: 311 us; the launch traced here: 310 us
  waiting for transfers between devices  177 us (57%)
  local copies, waits for them, and re-layouts  85.6 us (28%)
  other arithmetic  22.7 us (7%)
  between operations  13.5 us (4%)
  matrix products  10.3 us (3%)
    all_gather x1, waiting for transfers between devices, encode(): full_rows = lax.all_gather(rows_local, 'mp', axis=1, tiled=True)  95 us
    reduce_scatter x1, waiting for transfers between devices, encode(): lax.psum_scatter(lax.dot_general(out_weight, heads_out, (((0,), (0,)), ((...  81.7 us
    convert_element_type x2, local copies, waits for them, and re-layouts, encode(): as_float = patch_rows.astype(jnp.float32)  39.7 us
    mul x1, local copies, waits for them, and re-layouts, encode(): mean_square = jnp.mean(as_float * as_float, axis=-1, keepdims=True)  24.5 us
    unnamed x14, local copies, waits for them, and re-layouts  13.1 us
    reduce_sum x1, other arithmetic, encode(): mean_square = jnp.mean(as_float * as_float, axis=-1, keepdims=True)  8.05 us
    mul x1, other arithmetic, encode(): mean_square = jnp.mean(as_float * as_float, axis=-1, keepdims=True)  7.13 us
  transfers between devices with their start and end apart: 2, of which 2 were waited for; matrix products, arithmetic and copies ran while one was open for 0% of the time, Pallas kernels for 0%

commit v1 on v0

v1 whole, which is shorter than its diff:
```python
import jax
import jax.numpy as jnp
from jax import lax
from jax.experimental import pallas as pl
from jax.experimental.pallas import tpu as pltpu
from jax.sharding import Mesh, PartitionSpec as P

HEADS = 16
HEAD_DIM = 80
WIN = 64
WIDTH = 1280
LANES = 128
QKV_ROWS = 3 * HEAD_DIM
HEAD_ROWS = QKV_ROWS + HEAD_DIM
TILE_ROWS = 8
CHUNKS = WIDTH // LANES
PIECES = 64
PIECE_TILES = 7
PIECE_ROWS = PIECE_TILES * TILE_ROWS
SLAB_ROWS = PIECES * PIECE_ROWS
HEAD_STEP = 4
epsilon = 1e-06


def piece_kernel(index_ref, gain_ref, qkv_ref, out_ref, piece_ref):
    tiles_per_chunk = HEAD_ROWS // TILE_ROWS
    for step in range(PIECE_TILES):
        tile = index_ref[0] * PIECE_TILES + step
        tile = jnp.minimum(tile, CHUNKS * tiles_per_chunk - 1)
        chunk = tile // tiles_per_chunk
        row = (tile - chunk * tiles_per_chunk) * TILE_ROWS
        column = pl.multiple_of(chunk * LANES, LANES)
        rows = pl.ds(step * TILE_ROWS, TILE_ROWS)

        @pl.when(row < QKV_ROWS)
        def _():
            block = qkv_ref[pl.ds(pl.multiple_of(row, TILE_ROWS), TILE_ROWS), pl.ds(column, LANES)]
            gain = gain_ref[:, pl.ds(column, LANES)]
            piece_ref[rows, :] = (block.astype(jnp.float32) * gain).astype(jnp.bfloat16)

        @pl.when(row >= QKV_ROWS)
        def _():
            below = pl.multiple_of(row - QKV_ROWS, TILE_ROWS)
            piece_ref[rows, :] = out_ref[pl.ds(below, TILE_ROWS), pl.ds(column, LANES)]


def weight_piece(index, norm_gain, qkv_t, out_weight):
    vmem = pl.BlockSpec(memory_space=pltpu.VMEM)
    return pl.pallas_call(
        piece_kernel,
        out_shape=jax.ShapeDtypeStruct((PIECE_ROWS, LANES), jnp.bfloat16),
        in_specs=[pl.BlockSpec(memory_space=pltpu.SMEM), vmem, vmem, vmem],
        out_specs=vmem,
    )(index, norm_gain, qkv_t, out_weight)


def flat(ref):
    return ref.reshape(SLAB_ROWS, LANES)


def attend_kernel(live_ref, x_ref, *refs):
    slab_refs, (o_ref, out_sc, heads_sc) = refs[:HEAD_STEP], refs[HEAD_STEP:]
    step = pl.program_id(0)
    x = x_ref[...]
    xf = x.astype(jnp.float32)
    scale = lax.rsqrt(jnp.sum(xf * xf, axis=0, keepdims=True) * (1.0 / WIDTH) + epsilon)
    lane = lax.broadcasted_iota(jnp.int32, (WIN, LANES), 1)
    first = lane < WIN
    for local in range(HEAD_STEP):
        slab = flat(slab_refs[local])
        projected = None
        for pair in range(CHUNKS // 2):
            base = 2 * pair * HEAD_ROWS
            weights = jnp.concatenate(
                [slab[base:base + QKV_ROWS, :], slab[base + HEAD_ROWS:base + HEAD_ROWS + QKV_ROWS, :]], axis=1)
            term = jnp.dot(weights, x[2 * pair * LANES:2 * (pair + 1) * LANES, :],
                           preferred_element_type=jnp.float32)
            projected = term if projected is None else projected + term
        projected = (projected * scale).astype(jnp.bfloat16)
        queries = projected[:HEAD_DIM]
        keys = projected[HEAD_DIM:2 * HEAD_DIM]
        values = projected[2 * HEAD_DIM:]
        scores = lax.dot_general(keys, queries, (((0,), (0,)), ((), ())), preferred_element_type=jnp.float32)
        scores = jnp.where(first, scores[:WIN], scores[WIN:]) * HEAD_DIM ** (-0.5)
        scores = jnp.exp(scores - jnp.max(scores, axis=0, keepdims=True))
        probs = scores / jnp.sum(scores, axis=0, keepdims=True)
        zero = jnp.zeros_like(probs)
        probs = jnp.concatenate([jnp.where(first, probs, zero), jnp.where(first, zero, probs)], axis=0)
        out = jnp.dot(values, probs.astype(jnp.bfloat16), preferred_element_type=jnp.float32)
        rows = pl.ds(pl.multiple_of((step * HEAD_STEP + local) * HEAD_DIM, 16), HEAD_DIM)
        heads_sc[rows, :] = out.astype(jnp.bfloat16)
        for chunk in range(CHUNKS):
            base = chunk * HEAD_ROWS + QKV_ROWS
            out_sc[rows, chunk * LANES:(chunk + 1) * LANES] = slab[base:base + HEAD_DIM, :]

    @pl.when(step == pl.num_programs(0) - 1)
    def _():
        partial = lax.dot_general(heads_sc[...], out_sc[...], (((0,), (0,)), ((), ())),
                                  preferred_element_type=jnp.float32)
        total = xf + partial.T
        row_lane = lax.broadcasted_iota(jnp.int32, (1, LANES), 1)
        live = jnp.where(row_lane < WIN, live_ref[0], live_ref[1]) >= 0
        o_ref[...] = jnp.where(live, total, 0.0).astype(jnp.bfloat16)


def attend(live, x, slabs):
    return pl.pallas_call(
        attend_kernel,
        grid=(HEADS // HEAD_STEP,),
        out_shape=jax.ShapeDtypeStruct((WIDTH, LANES), jnp.bfloat16),
        in_specs=[
            pl.BlockSpec(memory_space=pltpu.SMEM),
            pl.BlockSpec((WIDTH, LANES), lambda i: (0, 0)),
        ] + [
            pl.BlockSpec((PIECES, None, PIECE_ROWS, LANES), lambda i, local=local: (0, HEAD_STEP * i + local, 0, 0))
            for local in range(HEAD_STEP)
        ],
        out_specs=pl.BlockSpec((WIDTH, LANES), lambda i: (0, 0)),
        scratch_shapes=[pltpu.VMEM((WIDTH, WIDTH), jnp.bfloat16), pltpu.VMEM((WIDTH, LANES), jnp.bfloat16)],
        compiler_params=pltpu.CompilerParams(vmem_limit_bytes=48 << 20),
    )(live, x, *([slabs] * HEAD_STEP))


def body(patches, norm_gain, qkv_weight, out_weight, window_plan):
    home = (lax.axis_index("x") * 8 + lax.axis_index("y")) * 2 + lax.axis_index("c")
    spot = lax.axis_index("z")
    piece = weight_piece(home.reshape(1).astype(jnp.int32), norm_gain.reshape(1, WIDTH), qkv_weight.T, out_weight)
    slabs = lax.all_gather(piece, ("x", "y", "c", "z"), axis=0, tiled=True)
    slabs = slabs.reshape(PIECES, HEADS, PIECE_ROWS, LANES)
    share = patches.shape[1] // WIN
    pairs = patches.reshape(16, 2, share, WIN).transpose(0, 2, 1, 3).reshape(16, share, LANES)
    mine = lax.all_to_all(pairs, "z", 0, 0, tiled=True).reshape(WIDTH, LANES)
    live = lax.dynamic_slice(window_plan, (home, spot * 2), (1, 2))[0]
    done = attend(live, mine, slabs).reshape(16, share, LANES)
    back = lax.all_to_all(done, "z", 0, 0, tiled=True)
    return back.reshape(16, share, 2, WIN).transpose(0, 2, 1, 3).reshape(32, share * WIN)


def solution(mesh):
    grid = Mesh(mesh.devices.reshape(4, 8, 2, 16), ("x", "y", "c", "z"))
    home = ("x", "y", "c")
    return jax.shard_map(
        body,
        mesh=grid,
        in_specs=(P(home, "z"), P(), P(None, "z"), P("z", None), P()),
        out_specs=P(home, "z"),
        check_vma=False,
    )
```

time: 311 us -> 300 us (0.965)
  the two profiles are of different devices: /device:TPU:2 before, /device:TPU:8 now
where the time goes in v1:
time: 300 us
  waiting for transfers between devices  219 us (73%)
  blocking collectives  28.3 us (9%)
  starting transfers between devices  18.9 us (6%)
  Pallas kernels  14.3 us (5%)
  between operations  13.4 us (4%)
  local copies, waits for them, and re-layouts  5.91 us (2%)
    all_gather x1, waiting for transfers between devices, body(): slabs = lax.all_gather(piece, ('x', 'y', 'c', 'z'), axis=0, tiled=True)  199 us
    all_to_all x1, blocking collectives, body(): back = lax.all_to_all(done, 'z', 0, 0, tiled=True)  28.3 us
    all_to_all x1, waiting for transfers between devices, body(): mine = lax.all_to_all(pairs, 'z', 0, 0, tiled=True).reshape(WIDTH, LANES)  20.7 us
    all_to_all x1, starting transfers between devices, body(): mine = lax.all_to_all(pairs, 'z', 0, 0, tiled=True).reshape(WIDTH, LANES)  18.9 us
    pallas_call x1, Pallas kernels, attend(): pl.pallas_call(attend_kernel, grid=(HEADS // HEAD_STEP,), out_shape=jax.S...  12.5 us
  transfers between devices with their start and end apart: 2, of which 2 were waited for; matrix products, arithmetic and copies ran while one was open for 1% of the time, Pallas kernels for 0%

profile of v1, /device:TPU:8, one launch (start us, length us, event | category | flops | bytes accessed | tf_op | source)
XLA Modules:
  0.0 300.1 jit_solution(13110060431292364613)
XLA Ops:
  6.5 0.0 copy-start
  6.5 0.0 all-gather.2.cloned.1.call-start
  6.5 1.3 reshape.31.gain_ref
  7.8 1.9 shard_map.55
  9.7 0.0 all-gather.2.cloned.1.call-update
  9.7 1.4 reshape.27
  11.2 0.3 copy.12
  11.5 0.9 copy.13
  12.4 18.9 %all-to-all-start = ((bf16[16,80,128]{2,1,0:T(8,128)(2,1)}), bf16[16,80,128]{2,1,0:T(8,128)(2,1)S(1)}, u32[]{:S(2)}, u32[]{:S(2)}) async-start(bf16[16,80,128]{2,1,0:T(8,128)(2,1)} %copy.13), calls=%async_computation | async-start | bytes 655360 | tf_op jit(solution)/shard_map/all_to_all | solution.py:132
  31.3 0.0 copy-done
  31.3 0.2 dynamic-slice_reduce_fusion.live_ref
  31.5 20.7 %all-to-all-done = bf16[16,80,128]{2,1,0:T(8,128)(2,1)S(1)} async-done(((bf16[16,80,128]{2,1,0:T(8,128)(2,1)}), bf16[16,80,128]{2,1,0:T(8,128)(2,1)S(1)}, u32[]{:S(2)}, u32[]{:S(2)}) %all-to-all-start) | async-done | bytes 327712 | tf_op jit(solution)/shard_map/all_to_all | solution.py:132
  52.1 198.6 %all-gather.2.cloned.1.call-done = bf16[57344,128]{1,0:T(8,128)(2,1)} async-done(((bf16[56,128]{1,0:T(8,128)(2,1)}), bf16[57344,128]{1,0:T(8,128)(2,1)}) %all-gather.2.cloned.1.call-update) | async-done | bytes 14680080 | tf_op jit(solution)/shard_map/all_gather | solution.py:128
  250.7 12.5 %shard_map.56 = bf16[1280,128]{1,0:T(8,128)(2,1)S(1)} custom-call(s32[2]{0:T(128)S(1)} %dynamic-slice_reduce_fusion.live_ref, bf16[1280,128]{1,0:T(8,128)(2,1)S(1)} %bitcast.12, bf16[64,16,56,128]{3,2,1,0:T(8,128)(2,1)} %bitcast.14, bf16[64,16,56,128]{3,2,1,0:T(8,128)(2,1)} %bitcast.15, bf16[64,16,56,128]{3,2,1,0:T(8,128)(2,1)} %bitcast.16, ...), custom_call_target="tpu_custom_call" | custom-call | tf_op jit(solution)/shard_map/pallas_call | solution.py:107
  263.2 28.3 %all_to_all.10 = bf16[16,80,128]{2,1,0:T(8,128)(2,1)S(1)} all-to-all(bf16[16,80,128]{2,1,0:T(8,128)(2,1)S(1)} %bitcast.13), channel_id=1, replica_groups=mesh['x'=4,'y'=8,'c'=2,'z'=16] {'z'}, dimensions={0} | all-to-all | bytes 655360 | tf_op jit(solution)/shard_map/all_to_all | solution.py:135
  291.5 0.3 copy.14
  291.8 0.3 copy.15
  292.1 1.2 reshape.35
Async XLA Ops:
  6.5 24.7 %copy-start = (s32[64,32]{0,1:T(8,128)S(1)}, s32[64,32]{0,1:T(8,128)}, u32[]{:S(2)}) copy-start(s32[64,32]{0,1:T(8,128)} %param.9) | copy-start | bytes 24580
  6.5 244.2 %all-gather.2.cloned.1.call-start = ((), (), s32[]{:S(2)}) async-start(), calls=%async_computation.2 | async-start | bytes 14694400 | tf_op jit(solution)/shard_map/all_gather | solution.py:128
  12.4 39.7 %all-to-all-start = ((bf16[16,80,128]{2,1,0:T(8,128)(2,1)}), bf16[16,80,128]{2,1,0:T(8,128)(2,1)S(1)}, u32[]{:S(2)}, u32[]{:S(2)}) async-start(bf16[16,80,128]{2,1,0:T(8,128)(2,1)} %copy.13), calls=%async_computation | async-start | bytes 655360 | tf_op jit(solution)/shard_map/all_to_all | solution.py:132
Sparse Core Ops, SparseCore 0:
  13.1 237.5 all-gather.1
